TPU v7x, 512 devices: a whole 4x4x16 slice. The times are simulated.
512 devices in a mesh: occ: 64 (over z_lo, y, core), aux: 8 (over x, z_hi).
Axes of the slice: x: 4, y: 4, z: 16 (z_hi: 2, z_lo: 8; z = z_hi * 8 + z_lo), core: 2. Of those that a mesh axis runs over, the one named last changes fastest.
Arguments:
- half_blocks: bfloat16 [1536, 64, 6144], P('occ', None, 'aux'), may hold values from -0.796875 to 0.796875
- block_rows: int32 [64], replicated, may hold values from 1 to 24, 768 in all
- block_order: int32 [64], replicated, may hold values from 0 to 63, each once
- ao_to_virt: bfloat16 [768, 512], replicated, may hold values from -0.21875 to 0.21875
- occ_energy: float32 [64], replicated, may hold values from -2 to -0.5
- virt_energy: float32 [512], replicated, may hold values from 0.2 to 3
Outputs:
- gamma: float32 [64, 512, 6144], P('occ', None, 'aux')
Inputs may be any that keep to these rules, and one draw needn't show every extreme that they name: block_rows[s] is the number of AO functions held by device s of occ; the counts sum to 768 and one of them equals 24. A permutation; the runs of AO functions lie end to end in the order of block_order.
All inputs are finite; a program needn't handle non-finite values.
Results may differ from a plain program's by a relative error of at most 0.008.
Values may be sent and summed in bfloat16 or wider, within the bound.
No kernel may reach another device: no remote copies, remote signals or barrier semaphores. Data moves between devices by JAX's collectives and lax.ppermute only.
A program may use at most 64 MiB of HBM per device.

v0:
```python
import functools
import math

import jax
import jax.numpy as jnp
from jax import lax
from jax.experimental import pallas as pl
from jax.experimental.pallas import tpu as pltpu
from jax.sharding import PartitionSpec as P


XS = 4
ZS = 2
PLANE = 8
DIRECT = 8
STEADY = 80


def shifted(value, axis, by):
    devices = lax.axis_size(axis)
    return lax.ppermute(value, axis, [(i, (i + by) % devices) for i in range(devices)])


def exchanged_x(value):
    groups = [[x * ZS + z for x in range(XS)] for z in range(ZS)]
    return lax.all_to_all(value, "aux", 0, 0, axis_index_groups=groups, tiled=True)


def swapped_z(value):
    perm = [(x * ZS + z, x * ZS + 1 - z) for x in range(XS) for z in range(ZS)]
    return lax.ppermute(value, "aux", perm)


def crossed(value, mask):
    devices = lax.axis_size("occ")
    return lax.ppermute(value, "occ", [(i, i ^ mask) for i in range(devices)])


def picked(table, index):
    hot = index[:, None] == jnp.arange(table.shape[0], dtype=jnp.int32)[None, :]
    hot = hot.reshape(hot.shape + (1,) * (table.ndim - 1))
    return jnp.sum(jnp.where(hot, table[None], 0), axis=1)


def exclusive_sum(value):
    place = jnp.arange(value.shape[-1], dtype=jnp.int32)
    ahead = place[None, :] < place[:, None]
    return jnp.sum(jnp.where(ahead, value[..., None, :], 0), axis=-1)


def row_layout(block_rows, block_order, maxrows, plane):
    devices = block_rows.shape[0]
    numbers = jnp.arange(devices, dtype=jnp.int32)
    matches = block_order[:, None] == numbers[None, :]
    ordered = jnp.sum(jnp.where(matches, block_rows[None, :], 0), axis=1)
    starts = jnp.sum(jnp.where(matches, exclusive_sum(ordered)[:, None], 0), axis=0)
    offset = jnp.arange(DIRECT, dtype=jnp.int32)
    direct = jnp.where(offset[None, :] < block_rows[:, None], starts[:, None] + offset[None, :], -1)
    rest = jnp.maximum(block_rows - DIRECT, 0).reshape(-1, PLANE)
    first = exclusive_sum(rest)
    slots = jnp.arange(PLANE * (maxrows - DIRECT), dtype=jnp.int32)
    inside = (slots >= first[..., None]) & (slots < (first + rest)[..., None])
    source = (starts.reshape(-1, PLANE) + DIRECT - first)[..., None] + slots
    packed = jnp.sum(jnp.where(inside, source + 1, 0), axis=1) - 1
    packed = picked(packed, plane ^ jnp.arange(packed.shape[0], dtype=jnp.int32))
    targets = jnp.concatenate(
        [direct.reshape(-1), packed[:, :STEADY].reshape(-1), packed[:, STEADY:].reshape(-1)]
    )
    return targets, jnp.max(jnp.sum(rest, axis=1))


def table_of(targets, ao_to_virt):
    functions = jnp.arange(ao_to_virt.shape[0], dtype=jnp.int32)
    hot = (functions[:, None] == targets[None, :]).astype(jnp.bfloat16)
    return lax.dot_general(
        ao_to_virt, hot, (((0,), (0,)), ((), ())), preferred_element_type=jnp.float32
    ).astype(jnp.bfloat16)


NT = (((1,), (1,)), ((), ()))
IN_VMEM = pl.BlockSpec(memory_space=pltpu.VMEM)
IN_SMEM = pl.BlockSpec(memory_space=pltpu.SMEM)


def grant(mib):
    return pltpu.CompilerParams(vmem_limit_bytes=mib << 20)


def turn_kernel(rows_ref, out_ref):
    for low in range(0, out_ref.shape[0], PLANE):
        out_ref[low : low + PLANE] = pltpu.einshape("rdc->drc", rows_ref[:, low : low + PLANE, :])


def turned_rows(half_blocks):
    _, devices, columns = half_blocks.shape
    return pl.pallas_call(
        turn_kernel,
        grid=(1,),
        out_shape=jax.ShapeDtypeStruct((devices, DIRECT, columns), jnp.bfloat16),
        in_specs=[pl.BlockSpec((DIRECT, devices, columns), lambda i: (0, 0, 0))],
        out_specs=pl.BlockSpec((devices, DIRECT, columns), lambda i: (0, 0, 0)),
        compiler_params=grant(6),
        cost_estimate=pl.CostEstimate(
            flops=0, bytes_accessed=4 * DIRECT * devices * columns, transcendentals=0
        ),
    )(half_blocks)


def share_kernel(place_ref, rows_ref, *refs):
    outs, turned_ref = refs[:-1], refs[-1]
    planes = outs[0].shape[0]
    for plane in range(planes):
        block = rows_ref[:, plane * PLANE : (plane + 1) * PLANE, :]
        turned_ref[...] = pltpu.einshape("rdc->drc", block)
        for d, out_ref in enumerate(outs):
            out_ref[plane] = turned_ref[lax.bitwise_xor(place_ref[3], d)]


def shared_rows(place, rows):
    count, devices, columns = rows.shape
    return pl.pallas_call(
        share_kernel,
        out_shape=[
            jax.ShapeDtypeStruct((devices // PLANE, count, columns), jnp.bfloat16)
        ] * PLANE,
        in_specs=[IN_SMEM, IN_VMEM],
        out_specs=[IN_VMEM] * PLANE,
        scratch_shapes=[pltpu.VMEM((PLANE, count, columns), jnp.bfloat16)],
        compiler_params=grant(8),
        cost_estimate=pl.CostEstimate(flops=0, bytes_accessed=4 * rows.size, transcendentals=0),
    )(place, rows)


def pack_kernel(place_ref, counts_ref, *refs):
    received, outs = refs[:PLANE], refs[PLANE:-2]
    rows_ref, first_ref = refs[-2:]
    steady, over_ref = outs[:-1], outs[-1]
    rows = received[0].shape[1]
    here = place_ref[2] * PLANE
    so_far = jnp.int32(0)
    for member in range(PLANE):
        first_ref[member] = so_far
        so_far += jnp.maximum(counts_ref[here + member] - DIRECT, 0)
    slots = rows_ref.shape[0]
    slot = lax.broadcasted_iota(jnp.int32, (slots, slots), 0)
    column = lax.broadcasted_iota(jnp.int32, (slots, slots), 1)
    wanted = jnp.full((slots, slots), -1, jnp.int32)
    for d in range(PLANE):
        sender = lax.bitwise_xor(place_ref[3], d)
        row = column - d * rows
        held = (row >= 0) & (row < jnp.minimum(counts_ref[here + sender] - DIRECT, rows))
        wanted = jnp.where(held, first_ref[sender] + row, wanted)
    packing = jnp.where(slot == wanted, 1.0, 0.0).astype(rows_ref.dtype)
    for step in range(len(steady)):
        plane = lax.bitwise_xor(place_ref[2], step)
        for d, ref in enumerate(received):
            rows_ref[d * rows : (d + 1) * rows, :] = ref[plane]
        packed = jnp.dot(packing, rows_ref[...], preferred_element_type=jnp.float32)
        packed = packed.astype(rows_ref.dtype)
        steady[step][...] = packed[:STEADY]
        over_ref[step] = packed[STEADY:]


def packed_rows(place, counts, received):
    planes, rows, columns = received[0].shape
    slots = PLANE * rows
    return pl.pallas_call(
        pack_kernel,
        out_shape=[jax.ShapeDtypeStruct((STEADY, columns), jnp.bfloat16)] * planes
        + [jax.ShapeDtypeStruct((planes, slots - STEADY, columns), jnp.bfloat16)],
        in_specs=[IN_SMEM] * 2 + [IN_VMEM] * PLANE,
        out_specs=[IN_VMEM] * (planes + 1),
        scratch_shapes=[
            pltpu.VMEM((slots, columns), jnp.bfloat16),
            pltpu.SMEM((PLANE,), jnp.int32),
        ],
        compiler_params=grant(6),
        cost_estimate=pl.CostEstimate(
            flops=2 * planes * slots * slots * columns,
            bytes_accessed=4 * planes * slots * columns,
            transcendentals=0,
        ),
    )(place, counts, *received)


def tile_kernel(table_ref, direct_ref, *refs):
    steady, over_ref, out_ref, rows_ref = refs[:-3], refs[-3], refs[-2], refs[-1]
    count = direct_ref.shape[0]
    for step, ref in enumerate(steady):
        rows_ref[step * STEADY : (step + 1) * STEADY, :] = ref[...]
    done = len(steady) * STEADY
    rows_ref[done:, :] = over_ref[...]
    total = jnp.dot(table_ref[:, :count], direct_ref[...], preferred_element_type=jnp.float32)
    total += jnp.dot(table_ref[:, count:], rows_ref[...], preferred_element_type=jnp.float32)
    out_ref[...] = total.astype(out_ref.dtype)


def tile_of(table, direct, steady, over):
    vt, rows = table.shape
    columns = direct.shape[1]
    return pl.pallas_call(
        tile_kernel,
        out_shape=jax.ShapeDtypeStruct((vt, columns), jnp.bfloat16),
        in_specs=[IN_VMEM] * (3 + len(steady)),
        out_specs=IN_VMEM,
        scratch_shapes=[pltpu.VMEM((rows - direct.shape[0], columns), jnp.bfloat16)],
        compiler_params=grant(56),
        cost_estimate=pl.CostEstimate(
            flops=2 * vt * rows * columns,
            bytes_accessed=2 * (vt * rows + rows * columns + vt * columns),
            transcendentals=0,
        ),
    )(table, direct, *steady, over)


def own_tile_of(half_blocks, block_rows, block_order, ao_to_virt, place, position):
    maxrows, devices, columns = half_blocks.shape
    planes = devices // PLANE
    plane = position // PLANE
    direct = sent_to_owners(turned_rows(half_blocks))
    targets, most = row_layout(block_rows, block_order, maxrows, plane)
    table = table_of(targets, ao_to_virt)
    blocks = shared_rows(place, half_blocks[DIRECT:])
    received = [blocks[0]] + [crossed(blocks[d], d) for d in range(1, PLANE)]
    *steady, over = packed_rows(place, block_rows, received)
    arrived = [steady[0]] + [None] * (planes - 1)
    for m in sorted(range(1, planes), key=lambda m: (m < planes // 2, m)):
        arrived[m] = crossed(steady[m], m * PLANE)

    def overflow(rows):
        return jnp.stack([rows[0]] + [crossed(rows[m], m * PLANE) for m in range(1, planes)])

    over = lax.cond(most > STEADY, overflow, jnp.zeros_like, over)
    return tile_of(table, direct, arrived, over.reshape(-1, columns))


def sent_to_owners(rows):
    arrived = lax.all_to_all(rows, "occ", split_axis=0, concat_axis=0, tiled=True)
    return arrived.reshape(-1, rows.shape[2])


def pair_kernel(own_ref, *refs):
    others, out_ref = refs[:-1], refs[-1]
    copies, _, rows, _ = out_ref.shape
    for step in range(copies):
        block = pl.ds(step * rows, rows)
        for k, other_ref in enumerate(others):
            direct = lax.dot_general(
                own_ref[block, :], other_ref[...], NT, preferred_element_type=jnp.float32
            )
            crossed = lax.dot_general(
                other_ref[block, :], own_ref[...], NT, preferred_element_type=jnp.float32
            )
            out_ref[step, k] = (2.0 * direct - crossed).astype(out_ref.dtype)


def pair_blocks(own, others):
    vt, columns = own.shape
    count = len(others)
    return pl.pallas_call(
        pair_kernel,
        out_shape=jax.ShapeDtypeStruct((XS, count, vt // XS, vt), jnp.bfloat16),
        in_specs=[IN_VMEM] * (1 + count),
        out_specs=IN_VMEM,
        compiler_params=grant(4 + 2 * count),
        cost_estimate=pl.CostEstimate(
            flops=4 * count * vt * vt * columns,
            bytes_accessed=2 * (1 + count) * vt * columns + 2 * count * vt * vt,
            transcendentals=0,
        ),
    )(own, *others)


def sum_kernel(blocks_ref, out_ref):
    total = blocks_ref[0].astype(jnp.float32)
    for step in range(1, blocks_ref.shape[0]):
        total = total + blocks_ref[step].astype(jnp.float32)
    out_ref[...] = total.astype(out_ref.dtype)


def sum_of(blocks):
    return pl.pallas_call(
        sum_kernel,
        out_shape=jax.ShapeDtypeStruct(blocks.shape[1:], jnp.bfloat16),
        in_specs=[IN_VMEM],
        out_specs=IN_VMEM,
        compiler_params=grant(4),
        cost_estimate=pl.CostEstimate(
            flops=blocks.size, bytes_accessed=3 * blocks.size, transcendentals=0
        ),
    )(blocks)


def amplitude_kernel(groups, place_ref, energy_ref, column_ref, row_ref, *refs):
    parts, out_ref = refs[:-1], refs[-1]
    copies, _, rows, _ = out_ref.shape
    occupied = energy_ref.shape[0]
    position = place_ref[0]
    block = pl.ds(pl.multiple_of(place_ref[1] * rows, rows), rows)
    both = column_ref[block, :] + row_ref[...]
    done = 0
    for group, steps in enumerate(groups):
        one_ref, two_ref = parts[2 * group : 2 * group + 2]
        for k, step in enumerate(steps):
            partner = lax.rem(position + occupied - step, occupied)
            gap = both - energy_ref[position] - energy_ref[partner]
            merged = one_ref[k].astype(jnp.float32) + two_ref[k].astype(jnp.float32)
            amplitude = (merged / gap).astype(out_ref.dtype)
            for copy in range(copies):
                out_ref[copy, done + k] = amplitude
        done += len(steps)


def amplitude_of(groups, place, energies, column, row, parts):
    count = sum(len(steps) for steps in groups)
    shape = (XS, count) + parts[0][0].shape[1:]
    size = math.prod(shape[1:])
    return pl.pallas_call(
        functools.partial(amplitude_kernel, groups),
        out_shape=jax.ShapeDtypeStruct(shape, jnp.bfloat16),
        in_specs=[IN_SMEM] * 2 + [IN_VMEM] * (2 + 2 * len(groups)),
        out_specs=IN_VMEM,
        compiler_params=grant(6),
        cost_estimate=pl.CostEstimate(
            flops=6 * size, bytes_accessed=12 * size, transcendentals=0
        ),
    )(place, energies, column, row, *[array for pair in parts for array in pair])


def density_kernel(count, amplitude_ref, *refs):
    tiles, rest = refs[:count], refs[count:]
    tile_ref, sems = rest[-2:]
    out_ref = rest[-3]
    copies = [pltpu.make_async_copy(tiles[k], tile_ref.at[k], sems.at[k]) for k in range(count)]
    for copy in copies:
        copy.start()
    for copy in copies:
        copy.wait()
    steps, _, rows, _ = amplitude_ref.shape
    for step in range(steps):
        block = pl.ds(step * rows, rows)
        total = rest[0][block, :] if len(rest) > 3 else None
        for k in range(count):
            term = jnp.dot(
                amplitude_ref[step, k], tile_ref[k], preferred_element_type=jnp.float32
            )
            total = term if total is None else total + term
        out_ref[block, :] = total


def density_of(amplitudes, tiles, so_far=None):
    count = len(tiles)
    vt, columns = tiles[0].shape
    args = [amplitudes] + list(tiles)
    in_specs = [IN_VMEM] + [pl.BlockSpec(memory_space=pltpu.HBM)] * count
    aliases = {}
    if so_far is not None:
        aliases = {len(args): 0}
        args.append(so_far)
        in_specs.append(IN_VMEM)
    return pl.pallas_call(
        functools.partial(density_kernel, count),
        out_shape=jax.ShapeDtypeStruct((vt, columns), jnp.float32),
        in_specs=in_specs,
        out_specs=IN_VMEM,
        scratch_shapes=[
            pltpu.VMEM((count, vt, columns), jnp.bfloat16),
            pltpu.SemaphoreType.DMA((count,)),
        ],
        compiler_params=grant(14),
        input_output_aliases=aliases,
        cost_estimate=pl.CostEstimate(
            flops=2 * count * vt * vt * columns,
            bytes_accessed=4 * vt * columns + count * (2 * vt * columns + 2 * vt * vt),
            transcendentals=0,
        ),
    )(*args)


GROUPS = ((0,), (1, 2), (3,))
HALVES = ((0, 2), (2, 3))


def shards(half_blocks, block_rows, block_order, ao_to_virt, occ_energy, virt_energy):
    position = lax.axis_index("occ").astype(jnp.int32)
    place = jnp.stack(
        [
            position,
            lax.axis_index("aux").astype(jnp.int32) // ZS,
            position // PLANE,
            position % PLANE,
        ]
    )
    column, row = virt_energy[:, None], virt_energy[None, :]
    own_tile = own_tile_of(half_blocks, block_rows, block_order, ao_to_virt, place, position)
    tiles = [own_tile, shifted(own_tile, "occ", 1), shifted(own_tile, "occ", 2)]
    tiles.append(shifted(tiles[2], "occ", 1))
    parts = []
    for steps in GROUPS:
        blocks = pair_blocks(own_tile, [tiles[k] for k in steps])
        part = sum_of(exchanged_x(blocks))
        parts.append((part, swapped_z(part)))
    density = None
    for lo, hi in HALVES:
        amplitude = amplitude_of(GROUPS[lo:hi], place, occ_energy, column, row, parts[lo:hi])
        amplitude = exchanged_x(amplitude)
        steps = [k for group in GROUPS[lo:hi] for k in group]
        density = density_of(amplitude, [tiles[k] for k in steps], density)
    return density[None]


def solution(mesh):
    return jax.shard_map(
        shards,
        mesh=mesh,
        in_specs=(P("occ", None, "aux"), P(), P(), P(), P(), P()),
        out_specs=P("occ", None, "aux"),
        check_vma=False,
    )
```

profile of v0, /device:TPU:56, one launch (start us, length us, event | category | flops | bytes accessed | tf_op | source)
XLA Modules:
  0.0 271.3 jit_solution(5357934177261539219)
XLA Ops:
  2.8 15.7 %all-to-all-start = ((bf16[64,8,768]{2,1,0:T(8,128)(2,1)}), bf16[64,8,768]{2,1,0:T(8,128)(2,1)}, u32[]{:S(2)}, u32[]{:S(2)}) async-start(bf16[64,8,768]{2,1,0:T(8,128)(2,1)} %copy-done.5), calls=%async_computation | async-start | bytes 1572864 | tf_op jit(solution)/shard_map/all_to_all | solution.py:238
  22.2 3.4 %collective-permute-start.10 = (bf16[8,16,768]{2,1,0:T(8,128)(2,1)S(1)}, bf16[8,16,768]{2,1,0:T(8,128)(2,1)S(1)}, u32[]{:S(2)}, u32[]{:S(2)}) collective-permute-start(bf16[8,16,768]{2,1,0:T(8,128)(2,1)S(1)} %get-tuple-element.31), channel_id=1, source_target_pairs={{0,32},{8,40},{16,48},{24,56},{32,0},{40,8},{48,16},{56,24},{64,96... | collective-permute-start | bytes 589832 | tf_op jit(solution)/shard_map/ppermute | solution.py:36
  25.6 3.4 %collective-permute-start.11 = (bf16[8,16,768]{2,1,0:T(8,128)(2,1)S(1)}, bf16[8,16,768]{2,1,0:T(8,128)(2,1)S(1)}, u32[]{:S(2)}, u32[]{:S(2)}) collective-permute-start(bf16[8,16,768]{2,1,0:T(8,128)(2,1)S(1)} %get-tuple-element.32), channel_id=1, source_target_pairs={{0,40},{8,32},{16,56},{24,48},{32,8},{40,0},{48,24},{56,16},{64,10... | collective-permute-start | bytes 589832 | tf_op jit(solution)/shard_map/ppermute | solution.py:36
  31.5 4.6 %collective-permute-start.13 = (bf16[8,16,768]{2,1,0:T(8,128)(2,1)S(1)}, bf16[8,16,768]{2,1,0:T(8,128)(2,1)S(1)}, u32[]{:S(2)}, u32[]{:S(2)}) collective-permute-start(bf16[8,16,768]{2,1,0:T(8,128)(2,1)S(1)} %get-tuple-element.34), channel_id=1, source_target_pairs={{0,56},{8,48},{16,40},{24,32},{32,24},{40,16},{48,8},{56,0},{64,12... | collective-permute-start | bytes 589832 | tf_op jit(solution)/shard_map/ppermute | solution.py:36
  42.5 3.6 %collective-permute-start.9 = (bf16[8,16,768]{2,1,0:T(8,128)(2,1)S(1)}, bf16[8,16,768]{2,1,0:T(8,128)(2,1)S(1)}, u32[]{:S(2)}, u32[]{:S(2)}) collective-permute-start(bf16[8,16,768]{2,1,0:T(8,128)(2,1)S(1)} %get-tuple-element.30), channel_id=1, source_target_pairs={{0,24},{8,16},{16,8},{24,0},{32,56},{40,48},{48,40},{56,32},{64,88... | collective-permute-start | bytes 589832 | tf_op jit(solution)/shard_map/ppermute | solution.py:36
  50.6 3.5 %collective-permute-done.9.refs_3_ = bf16[8,16,768]{2,1,0:T(8,128)(2,1)S(1)} collective-permute-done((bf16[8,16,768]{2,1,0:T(8,128)(2,1)S(1)}, bf16[8,16,768]{2,1,0:T(8,128)(2,1)S(1)}, u32[]{:S(2)}, u32[]{:S(2)}) %collective-permute-start.9) | collective-permute-done | bytes 196640 | tf_op jit(solution)/shard_map/ppermute | solution.py:36
  57.6 3.2 %collective-permute-start.14 = (bf16[80,768]{1,0:T(8,128)(2,1)S(1)}, bf16[80,768]{1,0:T(8,128)(2,1)S(1)}, u32[]{:S(2)}, u32[]{:S(2)}) collective-permute-start(bf16[80,768]{1,0:T(8,128)(2,1)S(1)} %get-tuple-element.36), channel_id=1, source_target_pairs={{0,64},{8,72},{16,80},{24,88},{32,96},{40,104},{48,112},{56,120},{... | collective-permute-start | bytes 368648 | tf_op jit(solution)/shard_map/ppermute | solution.py:36
  60.8 4.3 %collective-permute-start.15 = (bf16[80,768]{1,0:T(8,128)(2,1)S(1)}, bf16[80,768]{1,0:T(8,128)(2,1)S(1)}, u32[]{:S(2)}, u32[]{:S(2)}) collective-permute-start(bf16[80,768]{1,0:T(8,128)(2,1)S(1)} %get-tuple-element.37), channel_id=1, source_target_pairs={{0,128},{8,136},{16,144},{24,152},{32,160},{40,168},{48,176},{56,1... | collective-permute-start | bytes 368648 | tf_op jit(solution)/shard_map/ppermute | solution.py:36
  68.0 7.1 %collective-permute-start.17 = (bf16[80,768]{1,0:T(8,128)(2,1)S(1)}, bf16[80,768]{1,0:T(8,128)(2,1)S(1)}, u32[]{:S(2)}, u32[]{:S(2)}) collective-permute-start(bf16[80,768]{1,0:T(8,128)(2,1)S(1)} %get-tuple-element.39), channel_id=1, source_target_pairs={{0,256},{8,264},{16,272},{24,280},{32,288},{40,296},{48,304},{56,3... | collective-permute-start | bytes 368648 | tf_op jit(solution)/shard_map/ppermute | solution.py:36
  77.9 8.5 %collective-permute-start.19 = (bf16[80,768]{1,0:T(8,128)(2,1)S(1)}, bf16[80,768]{1,0:T(8,128)(2,1)S(1)}, u32[]{:S(2)}, u32[]{:S(2)}) collective-permute-start(bf16[80,768]{1,0:T(8,128)(2,1)S(1)} %get-tuple-element.41), channel_id=1, source_target_pairs={{0,384},{8,392},{16,400},{24,408},{32,416},{40,424},{48,432},{56,4... | collective-permute-start | bytes 368648 | tf_op jit(solution)/shard_map/ppermute | solution.py:36
  92.2 10.8 %collective-permute-done.17.refs_4_ = bf16[80,768]{1,0:T(8,128)(2,1)S(1)} collective-permute-done((bf16[80,768]{1,0:T(8,128)(2,1)S(1)}, bf16[80,768]{1,0:T(8,128)(2,1)S(1)}, u32[]{:S(2)}, u32[]{:S(2)}) %collective-permute-start.17) | collective-permute-done | bytes 122912 | tf_op jit(solution)/shard_map/ppermute | solution.py:36
  103.0 10.4 %collective-permute-done.18.refs_5_ = bf16[80,768]{1,0:T(8,128)(2,1)S(1)} collective-permute-done((bf16[80,768]{1,0:T(8,128)(2,1)S(1)}, bf16[80,768]{1,0:T(8,128)(2,1)S(1)}, u32[]{:S(2)}, u32[]{:S(2)}) %collective-permute-start.18) | collective-permute-done | bytes 122912 | tf_op jit(solution)/shard_map/ppermute | solution.py:36
  114.1 4.3 %shard_map.67.own_ref.refs_0_ = bf16[512,768]{1,0:T(8,128)(2,1)} custom-call(bf16[512,1536]{1,0:T(8,128)(2,1)} %fusion.2.table_ref, bf16[512,768]{1,0:T(8,128)(2,1)} %bitcast.22.direct_ref, bf16[80,768]{1,0:T(8,128)(2,1)} %copy-done.13, bf16[80,768]{1,0:T(8,128)(2,1)} %copy-done.17, bf16[80,768]{1,0:T(8,128)(2,1)} %copy-done.18, bf16[80,768]{1,0:T(8,128)(2,1)} %copy-done.19, ...), custom_call_target="tpu_custom_call" | custom-call | flops 1207959552 | bytes 4718592 | tf_op jit(solution)/shard_map/pallas_call | solution.py:201
  118.4 5.2 %collective-permute-start.21 = (bf16[512,768]{1,0:T(8,128)(2,1)}, bf16[512,768]{1,0:T(8,128)(2,1)}, u32[]{:S(2)}, u32[]{:S(2)}) collective-permute-start(bf16[512,768]{1,0:T(8,128)(2,1)} %shard_map.67.own_ref.refs_0_), channel_id=1, source_target_pairs={{0,16},{8,24},{16,32},{24,40},{32,48},{40,56},{48,64},{56,72},{64,... | collective-permute-start | bytes 2359304 | tf_op jit(solution)/shard_map/ppermute | solution.py:21
  129.6 4.3 %all-to-all-start.3 = ((bf16[4,1,128,512]{3,2,1,0:T(8,128)(2,1)}), bf16[4,1,128,512]{3,2,1,0:T(8,128)(2,1)S(1)}, u32[]{:S(2)}, u32[]{:S(2)}) async-start(bf16[4,1,128,512]{3,2,1,0:T(8,128)(2,1)} %shard_map.71), calls=%async_computation.3 | async-start | bytes 1048576 | tf_op jit(solution)/shard_map/all_to_all | solution.py:26
  133.9 7.9 %collective-permute-done.21.refs_1_.refs_2_ = bf16[512,768]{1,0:T(8,128)(2,1)} collective-permute-done((bf16[512,768]{1,0:T(8,128)(2,1)}, bf16[512,768]{1,0:T(8,128)(2,1)}, u32[]{:S(2)}, u32[]{:S(2)}) %collective-permute-start.21) | collective-permute-done | bytes 786464 | tf_op jit(solution)/shard_map/ppermute | solution.py:21
  143.8 4.4 %collective-permute-done.25.refs_0_.refs_1_ = bf16[512,768]{1,0:T(8,128)(2,1)S(1)} collective-permute-done((bf16[512,768]{1,0:T(8,128)(2,1)}, bf16[512,768]{1,0:T(8,128)(2,1)S(1)}, u32[]{:S(2)}, u32[]{:S(2)}) %collective-permute-start.25) | collective-permute-done | bytes 786464 | tf_op jit(solution)/shard_map/ppermute | solution.py:21
  148.2 5.6 %shard_map.73 = bf16[4,2,128,512]{3,2,1,0:T(8,128)(2,1)S(1)} custom-call(bf16[512,768]{1,0:T(8,128)(2,1)S(1)} %copy-done.7, bf16[512,768]{1,0:T(8,128)(2,1)S(1)} %collective-permute-done.25.refs_0_.refs_1_, bf16[512,768]{1,0:T(8,128)(2,1)} %collective-permute-done.21.refs_1_.refs_2_), custom_call_target="tpu_custom_call" | custom-call | flops 1610612736 | bytes 3407872 | tf_op jit(solution)/shard_map/pallas_call | solution.py:260
  154.8 4.3 %all-to-all-start.4 = ((bf16[4,2,128,512]{3,2,1,0:T(8,128)(2,1)}), bf16[4,2,128,512]{3,2,1,0:T(8,128)(2,1)S(1)}, u32[]{:S(2)}, u32[]{:S(2)}) async-start(bf16[4,2,128,512]{3,2,1,0:T(8,128)(2,1)} %copy-done.9), calls=%async_computation.4 | async-start | bytes 2097152 | tf_op jit(solution)/shard_map/all_to_all | solution.py:26
  159.1 3.3 %shard_map.68 = bf16[4,1,128,512]{3,2,1,0:T(8,128)(2,1)S(1)} custom-call(bf16[512,768]{1,0:T(8,128)(2,1)S(1)} %copy-done.7, bf16[512,768]{1,0:T(8,128)(2,1)} %collective-permute-done.22.refs_0_), custom_call_target="tpu_custom_call" | custom-call | flops 805306368 | bytes 2097152 | tf_op jit(solution)/shard_map/pallas_call | solution.py:260
  163.2 12.3 %all-to-all-done.4.blocks_ref = bf16[4,2,128,512]{3,2,1,0:T(8,128)(2,1)S(1)} async-done(((bf16[4,2,128,512]{3,2,1,0:T(8,128)(2,1)}), bf16[4,2,128,512]{3,2,1,0:T(8,128)(2,1)S(1)}, u32[]{:S(2)}, u32[]{:S(2)}) %all-to-all-start.4) | async-done | bytes 1048608 | tf_op jit(solution)/shard_map/all_to_all | solution.py:26
  175.5 4.1 %all-to-all-start.1 = ((bf16[4,1,128,512]{3,2,1,0:T(8,128)(2,1)}), bf16[4,1,128,512]{3,2,1,0:T(8,128)(2,1)}, u32[]{:S(2)}, u32[]{:S(2)}) async-start(bf16[4,1,128,512]{3,2,1,0:T(8,128)(2,1)} %copy-done.12), calls=%async_computation.1 | async-start | bytes 1048576 | tf_op jit(solution)/shard_map/all_to_all | solution.py:26
  179.8 8.2 %collective-permute-start.26 = (bf16[2,128,512]{2,1,0:T(8,128)(2,1)S(1)}, bf16[2,128,512]{2,1,0:T(8,128)(2,1)S(1)}, u32[]{:S(2)}, u32[]{:S(2)}) collective-permute-start(bf16[2,128,512]{2,1,0:T(8,128)(2,1)S(1)} %shard_map.74.refs_2_), channel_id=1, source_target_pairs={{0,1},{1,0},{2,3},{3,2},{4,5},{5,4},{6,7},{7,6},{8,9},{9,8},{10,11... | collective-permute-start | bytes 786440 | tf_op jit(solution)/shard_map/ppermute | solution.py:31
  188.1 6.3 %collective-permute-start.24 = (bf16[1,128,512]{2,1,0:T(8,128)(2,1)S(1)}, bf16[1,128,512]{2,1,0:T(8,128)(2,1)S(1)}, u32[]{:S(2)}, u32[]{:S(2)}) collective-permute-start(bf16[1,128,512]{2,1,0:T(8,128)(2,1)S(1)} %shard_map.72.refs_0_), channel_id=1, source_target_pairs={{0,1},{1,0},{2,3},{3,2},{4,5},{5,4},{6,7},{7,6},{8,9},{9,8},{10,11... | collective-permute-start | bytes 393224 | tf_op jit(solution)/shard_map/ppermute | solution.py:31
  194.6 32.3 %collective-permute-done.24.refs_1_ = bf16[1,128,512]{2,1,0:T(8,128)(2,1)S(1)} collective-permute-done((bf16[1,128,512]{2,1,0:T(8,128)(2,1)S(1)}, bf16[1,128,512]{2,1,0:T(8,128)(2,1)S(1)}, u32[]{:S(2)}, u32[]{:S(2)}) %collective-permute-start.24) | collective-permute-done | bytes 131104 | tf_op jit(solution)/shard_map/ppermute | solution.py:31
  228.8 4.5 %all-to-all-start.5 = ((bf16[4,3,128,512]{3,2,1,0:T(8,128)(2,1)}), bf16[4,3,128,512]{3,2,1,0:T(8,128)(2,1)S(1)}, u32[]{:S(2)}, u32[]{:S(2)}) async-start(bf16[4,3,128,512]{3,2,1,0:T(8,128)(2,1)} %copy-done.4), calls=%async_computation.5 | async-start | bytes 3145728 | tf_op jit(solution)/shard_map/all_to_all | solution.py:26
  234.4 8.3 %collective-permute-start.23 = (bf16[1,128,512]{2,1,0:T(8,128)(2,1)S(1)}, bf16[1,128,512]{2,1,0:T(8,128)(2,1)S(1)}, u32[]{:S(2)}, u32[]{:S(2)}) collective-permute-start(bf16[1,128,512]{2,1,0:T(8,128)(2,1)S(1)} %shard_map.69.refs_0_), channel_id=1, source_target_pairs={{0,1},{1,0},{2,3},{3,2},{4,5},{5,4},{6,7},{7,6},{8,9},{9,8},{10,11... | collective-permute-start | bytes 393224 | tf_op jit(solution)/shard_map/ppermute | solution.py:31
  242.8 7.2 %collective-permute-done.23.refs_1_ = bf16[1,128,512]{2,1,0:T(8,128)(2,1)S(1)} collective-permute-done((bf16[1,128,512]{2,1,0:T(8,128)(2,1)S(1)}, bf16[1,128,512]{2,1,0:T(8,128)(2,1)S(1)}, u32[]{:S(2)}, u32[]{:S(2)}) %collective-permute-start.23) | collective-permute-done | bytes 131104 | tf_op jit(solution)/shard_map/ppermute | solution.py:31
  254.0 4.1 %all-to-all-start.2 = ((bf16[4,1,128,512]{3,2,1,0:T(8,128)(2,1)}), bf16[4,1,128,512]{3,2,1,0:T(8,128)(2,1)}, u32[]{:S(2)}, u32[]{:S(2)}) async-start(bf16[4,1,128,512]{3,2,1,0:T(8,128)(2,1)} %copy-done.8), calls=%async_computation.2 | async-start | bytes 1048576 | tf_op jit(solution)/shard_map/all_to_all | solution.py:26
  259.2 3.8 %shard_map.76.refs_1_ = f32[512,768]{1,0:T(8,128)} custom-call(bf16[4,3,128,512]{3,2,1,0:T(8,128)(2,1)S(1)} %all-to-all-done.5.amplitude_ref, bf16[512,768]{1,0:T(8,128)(2,1)S(1)} %copy-done.7, bf16[512,768]{1,0:T(8,128)(2,1)S(1)} %copy-done.11, bf16[512,768]{1,0:T(8,128)(2,1)} %collective-permute-done.21.refs_1_.refs_2_), custom_call_target="tpu_custom_call" | custom-call | flops 1207959552 | bytes 5505024 | tf_op jit(solution)/shard_map/pallas_call | solution.py:361
  263.1 3.7 %all-to-all-done.2.amplitude_ref = bf16[4,1,128,512]{3,2,1,0:T(8,128)(2,1)} async-done(((bf16[4,1,128,512]{3,2,1,0:T(8,128)(2,1)}), bf16[4,1,128,512]{3,2,1,0:T(8,128)(2,1)}, u32[]{:S(2)}, u32[]{:S(2)}) %all-to-all-start.2) | async-done | bytes 524320 | tf_op jit(solution)/shard_map/all_to_all | solution.py:26
  266.7 4.4 %shard_map.77 = f32[512,768]{1,0:T(8,128)} custom-call(bf16[4,1,128,512]{3,2,1,0:T(8,128)(2,1)} %all-to-all-done.2.amplitude_ref, bf16[512,768]{1,0:T(8,128)(2,1)} %collective-permute-done.22.refs_0_, f32[512,768]{1,0:T(8,128)} %shard_map.76.refs_1_), custom_call_target="tpu_custom_call", output_to_operand_aliasing={{}: (2, {})} | custom-call | flops 402653184 | bytes 2883584 | tf_op jit(solution)/shard_map/pallas_call | solution.py:361
  (112 shorter events, 53.7 us)
Async XLA Ops:
  0.0 89.5 %copy-start = (bf16[768,512]{1,0:T(8,128)(2,1)S(1)}, bf16[768,512]{1,0:T(8,128)(2,1)}, u32[]{:S(2)}) copy-start(bf16[768,512]{1,0:T(8,128)(2,1)} %param.11) | copy-start | bytes 2359300
  2.8 110.6 %all-to-all-start = ((bf16[64,8,768]{2,1,0:T(8,128)(2,1)}), bf16[64,8,768]{2,1,0:T(8,128)(2,1)}, u32[]{:S(2)}, u32[]{:S(2)}) async-start(bf16[64,8,768]{2,1,0:T(8,128)(2,1)} %copy-done.5), calls=%async_computation | async-start | bytes 1572864 | tf_op jit(solution)/shard_map/all_to_all | solution.py:238
  19.8 18.5 %copy-start.24 = (s32[64]{0:T(128)S(1)}, s32[64]{0:T(128)}, u32[]{:S(2)}) copy-start(s32[64]{0:T(128)} %param.10) | copy-start | bytes 772
  22.2 18.4 %collective-permute-start.10 = (bf16[8,16,768]{2,1,0:T(8,128)(2,1)S(1)}, bf16[8,16,768]{2,1,0:T(8,128)(2,1)S(1)}, u32[]{:S(2)}, u32[]{:S(2)}) collective-permute-start(bf16[8,16,768]{2,1,0:T(8,128)(2,1)S(1)} %get-tuple-element.31), channel_id=1, source_target_pairs={{0,32},{8,40},{16,48},{24,56},{32,0},{40,8},{48,16},{56,24},{64,96... | collective-permute-start | bytes 589832 | tf_op jit(solution)/shard_map/ppermute | solution.py:36
  25.6 16.9 %collective-permute-start.11 = (bf16[8,16,768]{2,1,0:T(8,128)(2,1)S(1)}, bf16[8,16,768]{2,1,0:T(8,128)(2,1)S(1)}, u32[]{:S(2)}, u32[]{:S(2)}) collective-permute-start(bf16[8,16,768]{2,1,0:T(8,128)(2,1)S(1)} %get-tuple-element.32), channel_id=1, source_target_pairs={{0,40},{8,32},{16,56},{24,48},{32,8},{40,0},{48,24},{56,16},{64,10... | collective-permute-start | bytes 589832 | tf_op jit(solution)/shard_map/ppermute | solution.py:36
  29.0 17.2 %collective-permute-start.12 = (bf16[8,16,768]{2,1,0:T(8,128)(2,1)S(1)}, bf16[8,16,768]{2,1,0:T(8,128)(2,1)S(1)}, u32[]{:S(2)}, u32[]{:S(2)}) collective-permute-start(bf16[8,16,768]{2,1,0:T(8,128)(2,1)S(1)} %get-tuple-element.33), channel_id=1, source_target_pairs={{0,48},{8,56},{16,32},{24,40},{32,16},{40,24},{48,0},{56,8},{64,11... | collective-permute-start | bytes 589832 | tf_op jit(solution)/shard_map/ppermute | solution.py:36
  31.5 17.7 %collective-permute-start.13 = (bf16[8,16,768]{2,1,0:T(8,128)(2,1)S(1)}, bf16[8,16,768]{2,1,0:T(8,128)(2,1)S(1)}, u32[]{:S(2)}, u32[]{:S(2)}) collective-permute-start(bf16[8,16,768]{2,1,0:T(8,128)(2,1)S(1)} %get-tuple-element.34), channel_id=1, source_target_pairs={{0,56},{8,48},{16,40},{24,32},{32,24},{40,16},{48,8},{56,0},{64,12... | collective-permute-start | bytes 589832 | tf_op jit(solution)/shard_map/ppermute | solution.py:36
  36.1 13.1 %collective-permute-start.7 = (bf16[8,16,768]{2,1,0:T(8,128)(2,1)S(1)}, bf16[8,16,768]{2,1,0:T(8,128)(2,1)S(1)}, u32[]{:S(2)}, u32[]{:S(2)}) collective-permute-start(bf16[8,16,768]{2,1,0:T(8,128)(2,1)S(1)} %get-tuple-element.28), channel_id=1, source_target_pairs={{0,8},{8,0},{16,24},{24,16},{32,40},{40,32},{48,56},{56,48},{64,72... | collective-permute-start | bytes 589832 | tf_op jit(solution)/shard_map/ppermute | solution.py:36
  40.6 10.0 %collective-permute-start.8 = (bf16[8,16,768]{2,1,0:T(8,128)(2,1)S(1)}, bf16[8,16,768]{2,1,0:T(8,128)(2,1)S(1)}, u32[]{:S(2)}, u32[]{:S(2)}) collective-permute-start(bf16[8,16,768]{2,1,0:T(8,128)(2,1)S(1)} %get-tuple-element.29), channel_id=1, source_target_pairs={{0,16},{8,24},{16,0},{24,8},{32,48},{40,56},{48,32},{56,40},{64,80... | collective-permute-start | bytes 589832 | tf_op jit(solution)/shard_map/ppermute | solution.py:36
  42.5 11.6 %collective-permute-start.9 = (bf16[8,16,768]{2,1,0:T(8,128)(2,1)S(1)}, bf16[8,16,768]{2,1,0:T(8,128)(2,1)S(1)}, u32[]{:S(2)}, u32[]{:S(2)}) collective-permute-start(bf16[8,16,768]{2,1,0:T(8,128)(2,1)S(1)} %get-tuple-element.30), channel_id=1, source_target_pairs={{0,24},{8,16},{16,8},{24,0},{32,56},{40,48},{48,40},{56,32},{64,88... | collective-permute-start | bytes 589832 | tf_op jit(solution)/shard_map/ppermute | solution.py:36
  57.6 20.3 %collective-permute-start.14 = (bf16[80,768]{1,0:T(8,128)(2,1)S(1)}, bf16[80,768]{1,0:T(8,128)(2,1)S(1)}, u32[]{:S(2)}, u32[]{:S(2)}) collective-permute-start(bf16[80,768]{1,0:T(8,128)(2,1)S(1)} %get-tuple-element.36), channel_id=1, source_target_pairs={{0,64},{8,72},{16,80},{24,88},{32,96},{40,104},{48,112},{56,120},{... | collective-permute-start | bytes 368648 | tf_op jit(solution)/shard_map/ppermute | solution.py:36
  60.8 25.6 %collective-permute-start.15 = (bf16[80,768]{1,0:T(8,128)(2,1)S(1)}, bf16[80,768]{1,0:T(8,128)(2,1)S(1)}, u32[]{:S(2)}, u32[]{:S(2)}) collective-permute-start(bf16[80,768]{1,0:T(8,128)(2,1)S(1)} %get-tuple-element.37), channel_id=1, source_target_pairs={{0,128},{8,136},{16,144},{24,152},{32,160},{40,168},{48,176},{56,1... | collective-permute-start | bytes 368648 | tf_op jit(solution)/shard_map/ppermute | solution.py:36
  65.5 26.7 %collective-permute-start.16 = (bf16[80,768]{1,0:T(8,128)(2,1)S(1)}, bf16[80,768]{1,0:T(8,128)(2,1)S(1)}, u32[]{:S(2)}, u32[]{:S(2)}) collective-permute-start(bf16[80,768]{1,0:T(8,128)(2,1)S(1)} %get-tuple-element.38), channel_id=1, source_target_pairs={{0,192},{8,200},{16,208},{24,216},{32,224},{40,232},{48,240},{56,2... | collective-permute-start | bytes 368648 | tf_op jit(solution)/shard_map/ppermute | solution.py:36
  68.0 35.0 %collective-permute-start.17 = (bf16[80,768]{1,0:T(8,128)(2,1)S(1)}, bf16[80,768]{1,0:T(8,128)(2,1)S(1)}, u32[]{:S(2)}, u32[]{:S(2)}) collective-permute-start(bf16[80,768]{1,0:T(8,128)(2,1)S(1)} %get-tuple-element.39), channel_id=1, source_target_pairs={{0,256},{8,264},{16,272},{24,280},{32,288},{40,296},{48,304},{56,3... | collective-permute-start | bytes 368648 | tf_op jit(solution)/shard_map/ppermute | solution.py:36
  75.1 38.2 %collective-permute-start.18 = (bf16[80,768]{1,0:T(8,128)(2,1)S(1)}, bf16[80,768]{1,0:T(8,128)(2,1)S(1)}, u32[]{:S(2)}, u32[]{:S(2)}) collective-permute-start(bf16[80,768]{1,0:T(8,128)(2,1)S(1)} %get-tuple-element.40), channel_id=1, source_target_pairs={{0,320},{8,328},{16,336},{24,344},{32,352},{40,360},{48,368},{56,3... | collective-permute-start | bytes 368648 | tf_op jit(solution)/shard_map/ppermute | solution.py:36
  77.9 35.5 %collective-permute-start.19 = (bf16[80,768]{1,0:T(8,128)(2,1)S(1)}, bf16[80,768]{1,0:T(8,128)(2,1)S(1)}, u32[]{:S(2)}, u32[]{:S(2)}) collective-permute-start(bf16[80,768]{1,0:T(8,128)(2,1)S(1)} %get-tuple-element.41), channel_id=1, source_target_pairs={{0,384},{8,392},{16,400},{24,408},{32,416},{40,424},{48,432},{56,4... | collective-permute-start | bytes 368648 | tf_op jit(solution)/shard_map/ppermute | solution.py:36
  86.4 27.0 %collective-permute-start.20 = (bf16[80,768]{1,0:T(8,128)(2,1)S(1)}, bf16[80,768]{1,0:T(8,128)(2,1)S(1)}, u32[]{:S(2)}, u32[]{:S(2)}) collective-permute-start(bf16[80,768]{1,0:T(8,128)(2,1)S(1)} %get-tuple-element.42), channel_id=1, source_target_pairs={{0,448},{8,456},{16,464},{24,472},{32,480},{40,488},{48,496},{56,5... | collective-permute-start | bytes 368648 | tf_op jit(solution)/shard_map/ppermute | solution.py:36
  92.1 21.3 %copy-start.19 = (bf16[80,768]{1,0:T(8,128)(2,1)}, bf16[80,768]{1,0:T(8,128)(2,1)S(1)}, u32[]{:S(2)}) copy-start(bf16[80,768]{1,0:T(8,128)(2,1)S(1)} %collective-permute-done.16.refs_3_) | copy-start | bytes 368644
  118.4 23.4 %collective-permute-start.21 = (bf16[512,768]{1,0:T(8,128)(2,1)}, bf16[512,768]{1,0:T(8,128)(2,1)}, u32[]{:S(2)}, u32[]{:S(2)}) collective-permute-start(bf16[512,768]{1,0:T(8,128)(2,1)} %shard_map.67.own_ref.refs_0_), channel_id=1, source_target_pairs={{0,16},{8,24},{16,32},{24,40},{32,48},{40,56},{48,64},{56,72},{64,... | collective-permute-start | bytes 2359304 | tf_op jit(solution)/shard_map/ppermute | solution.py:21
  123.6 24.6 %collective-permute-start.25 = (bf16[512,768]{1,0:T(8,128)(2,1)}, bf16[512,768]{1,0:T(8,128)(2,1)S(1)}, u32[]{:S(2)}, u32[]{:S(2)}) collective-permute-start(bf16[512,768]{1,0:T(8,128)(2,1)} %shard_map.67.own_ref.refs_0_), channel_id=1, source_target_pairs={{0,8},{8,16},{16,24},{24,32},{32,40},{40,48},{48,56},{56,64},{64,7... | collective-permute-start | bytes 2359304 | tf_op jit(solution)/shard_map/ppermute | solution.py:21
  126.7 21.5 %copy-start.7 = (bf16[512,768]{1,0:T(8,128)(2,1)S(1)}, bf16[512,768]{1,0:T(8,128)(2,1)}, u32[]{:S(2)}) copy-start(bf16[512,768]{1,0:T(8,128)(2,1)} %shard_map.67.own_ref.refs_0_) | copy-start | bytes 2359300
  129.6 25.1 %all-to-all-start.3 = ((bf16[4,1,128,512]{3,2,1,0:T(8,128)(2,1)}), bf16[4,1,128,512]{3,2,1,0:T(8,128)(2,1)S(1)}, u32[]{:S(2)}, u32[]{:S(2)}) async-start(bf16[4,1,128,512]{3,2,1,0:T(8,128)(2,1)} %shard_map.71), calls=%async_computation.3 | async-start | bytes 1048576 | tf_op jit(solution)/shard_map/all_to_all | solution.py:26
  141.9 17.2 %collective-permute-start.22 = (bf16[512,768]{1,0:T(8,128)(2,1)}, bf16[512,768]{1,0:T(8,128)(2,1)}, u32[]{:S(2)}, u32[]{:S(2)}) collective-permute-start(bf16[512,768]{1,0:T(8,128)(2,1)} %collective-permute-done.21.refs_1_.refs_2_), channel_id=1, source_target_pairs={{0,8},{8,16},{16,24},{24,32},{32,40},{40,48},{48,56},{56,64},{64,7... | collective-permute-start | bytes 2359304 | tf_op jit(solution)/shard_map/ppermute | solution.py:21
  154.8 20.7 %all-to-all-start.4 = ((bf16[4,2,128,512]{3,2,1,0:T(8,128)(2,1)}), bf16[4,2,128,512]{3,2,1,0:T(8,128)(2,1)S(1)}, u32[]{:S(2)}, u32[]{:S(2)}) async-start(bf16[4,2,128,512]{3,2,1,0:T(8,128)(2,1)} %copy-done.9), calls=%async_computation.4 | async-start | bytes 2097152 | tf_op jit(solution)/shard_map/all_to_all | solution.py:26
  163.2 31.2 %copy-start.14 = (f32[512]{0:T(512)S(1)}, f32[512]{0:T(512)}, u32[]{:S(2)}) copy-start(f32[512]{0:T(512)} %param.13) | copy-start | bytes 6148
  163.2 63.6 %copy-start.16 = (f32[64]{0:T(128)S(1)}, f32[64]{0:T(128)}, u32[]{:S(2)}) copy-start(f32[64]{0:T(128)} %energy_ref.3) | copy-start | bytes 772
  175.5 53.3 %all-to-all-start.1 = ((bf16[4,1,128,512]{3,2,1,0:T(8,128)(2,1)}), bf16[4,1,128,512]{3,2,1,0:T(8,128)(2,1)}, u32[]{:S(2)}, u32[]{:S(2)}) async-start(bf16[4,1,128,512]{3,2,1,0:T(8,128)(2,1)} %copy-done.12), calls=%async_computation.1 | async-start | bytes 1048576 | tf_op jit(solution)/shard_map/all_to_all | solution.py:26
  179.8 47.1 %collective-permute-start.26 = (bf16[2,128,512]{2,1,0:T(8,128)(2,1)S(1)}, bf16[2,128,512]{2,1,0:T(8,128)(2,1)S(1)}, u32[]{:S(2)}, u32[]{:S(2)}) collective-permute-start(bf16[2,128,512]{2,1,0:T(8,128)(2,1)S(1)} %shard_map.74.refs_2_), channel_id=1, source_target_pairs={{0,1},{1,0},{2,3},{3,2},{4,5},{5,4},{6,7},{7,6},{8,9},{9,8},{10,11... | collective-permute-start | bytes 786440 | tf_op jit(solution)/shard_map/ppermute | solution.py:31
  188.1 38.7 %collective-permute-start.24 = (bf16[1,128,512]{2,1,0:T(8,128)(2,1)S(1)}, bf16[1,128,512]{2,1,0:T(8,128)(2,1)S(1)}, u32[]{:S(2)}, u32[]{:S(2)}) collective-permute-start(bf16[1,128,512]{2,1,0:T(8,128)(2,1)S(1)} %shard_map.72.refs_0_), channel_id=1, source_target_pairs={{0,1},{1,0},{2,3},{3,2},{4,5},{5,4},{6,7},{7,6},{8,9},{9,8},{10,11... | collective-permute-start | bytes 393224 | tf_op jit(solution)/shard_map/ppermute | solution.py:31
  228.8 25.2 %all-to-all-start.5 = ((bf16[4,3,128,512]{3,2,1,0:T(8,128)(2,1)}), bf16[4,3,128,512]{3,2,1,0:T(8,128)(2,1)S(1)}, u32[]{:S(2)}, u32[]{:S(2)}) async-start(bf16[4,3,128,512]{3,2,1,0:T(8,128)(2,1)} %copy-done.4), calls=%async_computation.5 | async-start | bytes 3145728 | tf_op jit(solution)/shard_map/all_to_all | solution.py:26
  234.4 15.6 %collective-permute-start.23 = (bf16[1,128,512]{2,1,0:T(8,128)(2,1)S(1)}, bf16[1,128,512]{2,1,0:T(8,128)(2,1)S(1)}, u32[]{:S(2)}, u32[]{:S(2)}) collective-permute-start(bf16[1,128,512]{2,1,0:T(8,128)(2,1)S(1)} %shard_map.69.refs_0_), channel_id=1, source_target_pairs={{0,1},{1,0},{2,3},{3,2},{4,5},{5,4},{6,7},{7,6},{8,9},{9,8},{10,11... | collective-permute-start | bytes 393224 | tf_op jit(solution)/shard_map/ppermute | solution.py:31
  254.0 12.8 %all-to-all-start.2 = ((bf16[4,1,128,512]{3,2,1,0:T(8,128)(2,1)}), bf16[4,1,128,512]{3,2,1,0:T(8,128)(2,1)}, u32[]{:S(2)}, u32[]{:S(2)}) async-start(bf16[4,1,128,512]{3,2,1,0:T(8,128)(2,1)} %copy-done.8), calls=%async_computation.2 | async-start | bytes 1048576 | tf_op jit(solution)/shard_map/all_to_all | solution.py:26
  (19 other events, 83.9 us)
where the time goes:
time: 273 us; the launch traced here: 271 us
  starting transfers between devices  122 us (45%)
  waiting for transfers between devices  99.4 us (36%)
  Pallas kernels  30.3 us (11%)
  local copies, waits for them, and re-layouts  14.1 us (5%)
    ppermute x14, starting transfers between devices, crossed(): return lax.ppermute(value, 'occ', [(i, i ^ mask) for i in range(devices)])  52.8 us
    ppermute x3, waiting for transfers between devices, swapped_z(): return lax.ppermute(value, 'aux', perm)  39.5 us
    ppermute x14, waiting for transfers between devices, crossed(): return lax.ppermute(value, 'occ', [(i, i ^ mask) for i in range(devices)])  29.1 us
    ppermute x3, starting transfers between devices, swapped_z(): return lax.ppermute(value, 'aux', perm)  22.9 us
    all_to_all x5, starting transfers between devices, exchanged_x(): lax.all_to_all(value, 'aux', 0, 0, axis_index_groups=groups, tiled=True)  21.4 us
    all_to_all x5, waiting for transfers between devices, exchanged_x(): lax.all_to_all(value, 'aux', 0, 0, axis_index_groups=groups, tiled=True)  18.5 us
    all_to_all x1, starting transfers between devices, sent_to_owners(): lax.all_to_all(rows, 'occ', split_axis=0, concat_axis=0, tiled=True)  15.7 us
    ppermute x3, waiting for transfers between devices, shifted(): lax.ppermute(value, axis, [(i, (i + by) % devices) for i in range(devices)])  12.4 us
  transfers between devices with their start and end apart: 26, of which 12 were waited for; matrix products, arithmetic and copies ran while one was open for 3% of the time, Pallas kernels for 8%

commit v1 on v0

--- a/solution.py
+++ b/solution.py
@@ -13,7 +13,7 @@
 ZS = 2
 PLANE = 8
 DIRECT = 8
-STEADY = 80
+STEADY = 88
 
 
 def shifted(value, axis, by):
@@ -242,16 +242,16 @@
 def pair_kernel(own_ref, *refs):
     others, out_ref = refs[:-1], refs[-1]
     copies, _, rows, _ = out_ref.shape
-    for step in range(copies):
-        block = pl.ds(step * rows, rows)
-        for k, other_ref in enumerate(others):
-            direct = lax.dot_general(
-                own_ref[block, :], other_ref[...], NT, preferred_element_type=jnp.float32
-            )
-            crossed = lax.dot_general(
-                other_ref[block, :], own_ref[...], NT, preferred_element_type=jnp.float32
-            )
-            out_ref[step, k] = (2.0 * direct - crossed).astype(out_ref.dtype)
+    for k, other_ref in enumerate(others):
+        direct = lax.dot_general(
+            own_ref[...], other_ref[...], NT, preferred_element_type=jnp.float32
+        )
+        crossed_over = lax.dot_general(
+            other_ref[...], own_ref[...], NT, preferred_element_type=jnp.float32
+        )
+        value = (2.0 * direct - crossed_over).astype(out_ref.dtype)
+        for step in range(copies):
+            out_ref[step, k] = value[step * rows : (step + 1) * rows]
 
 
 def pair_blocks(own, others):
@@ -336,16 +336,14 @@
         copy.start()
     for copy in copies:
         copy.wait()
-    steps, _, rows, _ = amplitude_ref.shape
-    for step in range(steps):
-        block = pl.ds(step * rows, rows)
-        total = rest[0][block, :] if len(rest) > 3 else None
-        for k in range(count):
-            term = jnp.dot(
-                amplitude_ref[step, k], tile_ref[k], preferred_element_type=jnp.float32
-            )
-            total = term if total is None else total + term
-        out_ref[block, :] = total
+    vt = out_ref.shape[0]
+    total = rest[0][...] if len(rest) > 3 else None
+    for k in range(count):
+        term = jnp.dot(
+            amplitude_ref[:, k].reshape(vt, vt), tile_ref[k], preferred_element_type=jnp.float32
+        )
+        total = term if total is None else total + term
+    out_ref[...] = total
 
 
 def density_of(amplitudes, tiles, so_far=None):

time: 273 us -> 273 us (level)
  Pallas kernels: 30.3 us -> 25.6 us
  waiting for transfers between devices: 99.4 us -> 104 us
    pallas_call x3, Pallas kernels: 11.8 us -> 7.19 us  [pair_blocks(): pl.pallas_call(pair_kernel, out_shape=jax.ShapeDtypeStruct((XS, count, vt...]
  transfers between devices with their start and end apart: 26 -> 26, of which waited for: 12 -> 10; matrix products, arithmetic and copies ran while one was open for 3% -> 3% of each run, Pallas kernels for 8% -> 6%
where the time goes in v1:
time: 273 us; the launch traced here: 271 us
  starting transfers between devices  122 us (45%)
  waiting for transfers between devices  104 us (38%)
  Pallas kernels  25.6 us (9%)
  local copies, waits for them, and re-layouts  14.1 us (5%)
    ppermute x14, starting transfers between devices, crossed(): return lax.ppermute(value, 'occ', [(i, i ^ mask) for i in range(devices)])  53.1 us
    ppermute x3, waiting for transfers between devices, swapped_z(): return lax.ppermute(value, 'aux', perm)  41.2 us
    ppermute x14, waiting for transfers between devices, crossed(): return lax.ppermute(value, 'occ', [(i, i ^ mask) for i in range(devices)])  31.6 us
    ppermute x3, starting transfers between devices, swapped_z(): return lax.ppermute(value, 'aux', perm)  22.9 us
    all_to_all x5, starting transfers between devices, exchanged_x(): lax.all_to_all(value, 'aux', 0, 0, axis_index_groups=groups, tiled=True)  21.7 us
    all_to_all x5, waiting for transfers between devices, exchanged_x(): lax.all_to_all(value, 'aux', 0, 0, axis_index_groups=groups, tiled=True)  18.2 us
    all_to_all x1, starting transfers between devices, sent_to_owners(): lax.all_to_all(rows, 'occ', split_axis=0, concat_axis=0, tiled=True)  15.7 us
    ppermute x3, waiting for transfers between devices, shifted(): lax.ppermute(value, axis, [(i, (i + by) % devices) for i in range(devices)])  12.6 us
  transfers between devices with their start and end apart: 26, of which 10 were waited for; matrix products, arithmetic and copies ran while one was open for 3% of the time, Pallas kernels for 6%

profile of v1, /device:TPU:56, one launch (start us, length us, event | category | flops | bytes accessed | tf_op | source)
XLA Modules:
  0.0 271.4 jit_solution(2213870154172541583)
XLA Ops:
  2.8 15.7 %all-to-all-start = ((bf16[64,8,768]{2,1,0:T(8,128)(2,1)}), bf16[64,8,768]{2,1,0:T(8,128)(2,1)}, u32[]{:S(2)}, u32[]{:S(2)}) async-start(bf16[64,8,768]{2,1,0:T(8,128)(2,1)} %copy-done.5), calls=%async_computation | async-start | bytes 1572864 | tf_op jit(solution)/shard_map/all_to_all | solution.py:238
  22.2 3.4 %collective-permute-start.10 = (bf16[8,16,768]{2,1,0:T(8,128)(2,1)S(1)}, bf16[8,16,768]{2,1,0:T(8,128)(2,1)S(1)}, u32[]{:S(2)}, u32[]{:S(2)}) collective-permute-start(bf16[8,16,768]{2,1,0:T(8,128)(2,1)S(1)} %get-tuple-element.31), channel_id=1, source_target_pairs={{0,32},{8,40},{16,48},{24,56},{32,0},{40,8},{48,16},{56,24},{64,96... | collective-permute-start | bytes 589832 | tf_op jit(solution)/shard_map/ppermute | solution.py:36
  25.6 3.4 %collective-permute-start.11 = (bf16[8,16,768]{2,1,0:T(8,128)(2,1)S(1)}, bf16[8,16,768]{2,1,0:T(8,128)(2,1)S(1)}, u32[]{:S(2)}, u32[]{:S(2)}) collective-permute-start(bf16[8,16,768]{2,1,0:T(8,128)(2,1)S(1)} %get-tuple-element.32), channel_id=1, source_target_pairs={{0,40},{8,32},{16,56},{24,48},{32,8},{40,0},{48,24},{56,16},{64,10... | collective-permute-start | bytes 589832 | tf_op jit(solution)/shard_map/ppermute | solution.py:36
  31.5 4.6 %collective-permute-start.13 = (bf16[8,16,768]{2,1,0:T(8,128)(2,1)S(1)}, bf16[8,16,768]{2,1,0:T(8,128)(2,1)S(1)}, u32[]{:S(2)}, u32[]{:S(2)}) collective-permute-start(bf16[8,16,768]{2,1,0:T(8,128)(2,1)S(1)} %get-tuple-element.34), channel_id=1, source_target_pairs={{0,56},{8,48},{16,40},{24,32},{32,24},{40,16},{48,8},{56,0},{64,12... | collective-permute-start | bytes 589832 | tf_op jit(solution)/shard_map/ppermute | solution.py:36
  41.2 3.6 %collective-permute-start.9 = (bf16[8,16,768]{2,1,0:T(8,128)(2,1)S(1)}, bf16[8,16,768]{2,1,0:T(8,128)(2,1)S(1)}, u32[]{:S(2)}, u32[]{:S(2)}) collective-permute-start(bf16[8,16,768]{2,1,0:T(8,128)(2,1)S(1)} %get-tuple-element.30), channel_id=1, source_target_pairs={{0,24},{8,16},{16,8},{24,0},{32,56},{40,48},{48,40},{56,32},{64,88... | collective-permute-start | bytes 589832 | tf_op jit(solution)/shard_map/ppermute | solution.py:36
  49.2 3.7 %collective-permute-done.9.refs_3_ = bf16[8,16,768]{2,1,0:T(8,128)(2,1)S(1)} collective-permute-done((bf16[8,16,768]{2,1,0:T(8,128)(2,1)S(1)}, bf16[8,16,768]{2,1,0:T(8,128)(2,1)S(1)}, u32[]{:S(2)}, u32[]{:S(2)}) %collective-permute-start.9) | collective-permute-done | bytes 196640 | tf_op jit(solution)/shard_map/ppermute | solution.py:36
  59.2 4.5 %collective-permute-start.15 = (bf16[88,768]{1,0:T(8,128)(2,1)S(1)}, bf16[88,768]{1,0:T(8,128)(2,1)S(1)}, u32[]{:S(2)}, u32[]{:S(2)}) collective-permute-start(bf16[88,768]{1,0:T(8,128)(2,1)S(1)} %get-tuple-element.37), channel_id=1, source_target_pairs={{0,128},{8,136},{16,144},{24,152},{32,160},{40,168},{48,176},{56,1... | collective-permute-start | bytes 405512 | tf_op jit(solution)/shard_map/ppermute | solution.py:36
  66.4 7.2 %collective-permute-start.17 = (bf16[88,768]{1,0:T(8,128)(2,1)S(1)}, bf16[88,768]{1,0:T(8,128)(2,1)S(1)}, u32[]{:S(2)}, u32[]{:S(2)}) collective-permute-start(bf16[88,768]{1,0:T(8,128)(2,1)S(1)} %get-tuple-element.39), channel_id=1, source_target_pairs={{0,256},{8,264},{16,272},{24,280},{32,288},{40,296},{48,304},{56,3... | collective-permute-start | bytes 405512 | tf_op jit(solution)/shard_map/ppermute | solution.py:36
  73.6 3.2 %collective-permute-start.18 = (bf16[88,768]{1,0:T(8,128)(2,1)S(1)}, bf16[88,768]{1,0:T(8,128)(2,1)S(1)}, u32[]{:S(2)}, u32[]{:S(2)}) collective-permute-start(bf16[88,768]{1,0:T(8,128)(2,1)S(1)} %get-tuple-element.40), channel_id=1, source_target_pairs={{0,320},{8,328},{16,336},{24,344},{32,352},{40,360},{48,368},{56,3... | collective-permute-start | bytes 405512 | tf_op jit(solution)/shard_map/ppermute | solution.py:36
  76.8 8.2 %collective-permute-start.19 = (bf16[88,768]{1,0:T(8,128)(2,1)S(1)}, bf16[88,768]{1,0:T(8,128)(2,1)S(1)}, u32[]{:S(2)}, u32[]{:S(2)}) collective-permute-start(bf16[88,768]{1,0:T(8,128)(2,1)S(1)} %get-tuple-element.41), channel_id=1, source_target_pairs={{0,384},{8,392},{16,400},{24,408},{32,416},{40,424},{48,432},{56,4... | collective-permute-start | bytes 405512 | tf_op jit(solution)/shard_map/ppermute | solution.py:36
  85.0 3.4 %collective-permute-start.20 = (bf16[88,768]{1,0:T(8,128)(2,1)S(1)}, bf16[88,768]{1,0:T(8,128)(2,1)S(1)}, u32[]{:S(2)}, u32[]{:S(2)}) collective-permute-start(bf16[88,768]{1,0:T(8,128)(2,1)S(1)} %get-tuple-element.42), channel_id=1, source_target_pairs={{0,448},{8,456},{16,464},{24,472},{32,480},{40,488},{48,496},{56,5... | collective-permute-start | bytes 405512 | tf_op jit(solution)/shard_map/ppermute | solution.py:36
  91.0 13.7 %collective-permute-done.17.refs_4_ = bf16[88,768]{1,0:T(8,128)(2,1)S(1)} collective-permute-done((bf16[88,768]{1,0:T(8,128)(2,1)S(1)}, bf16[88,768]{1,0:T(8,128)(2,1)S(1)}, u32[]{:S(2)}, u32[]{:S(2)}) %collective-permute-start.17) | collective-permute-done | bytes 135200 | tf_op jit(solution)/shard_map/ppermute | solution.py:36
  104.7 11.5 %collective-permute-done.18.refs_5_ = bf16[88,768]{1,0:T(8,128)(2,1)S(1)} collective-permute-done((bf16[88,768]{1,0:T(8,128)(2,1)S(1)}, bf16[88,768]{1,0:T(8,128)(2,1)S(1)}, u32[]{:S(2)}, u32[]{:S(2)}) %collective-permute-start.18) | collective-permute-done | bytes 135200 | tf_op jit(solution)/shard_map/ppermute | solution.py:36
  117.0 4.3 %shard_map.67.own_ref.refs_0_ = bf16[512,768]{1,0:T(8,128)(2,1)} custom-call(bf16[512,1536]{1,0:T(8,128)(2,1)} %fusion.2.table_ref, bf16[512,768]{1,0:T(8,128)(2,1)} %bitcast.22.direct_ref, bf16[88,768]{1,0:T(8,128)(2,1)} %copy-done.13, bf16[88,768]{1,0:T(8,128)(2,1)} %copy-done.17, bf16[88,768]{1,0:T(8,128)(2,1)} %copy-done.18, bf16[88,768]{1,0:T(8,128)(2,1)} %copy-done.19, ...), custom_call_target="tpu_custom_call" | custom-call | flops 1207959552 | bytes 4718592 | tf_op jit(solution)/shard_map/pallas_call | solution.py:201
  121.3 5.1 %collective-permute-start.21 = (bf16[512,768]{1,0:T(8,128)(2,1)}, bf16[512,768]{1,0:T(8,128)(2,1)}, u32[]{:S(2)}, u32[]{:S(2)}) collective-permute-start(bf16[512,768]{1,0:T(8,128)(2,1)} %shard_map.67.own_ref.refs_0_), channel_id=1, source_target_pairs={{0,16},{8,24},{16,32},{24,40},{32,48},{40,56},{48,64},{56,72},{64,... | collective-permute-start | bytes 2359304 | tf_op jit(solution)/shard_map/ppermute | solution.py:21
  131.3 4.3 %all-to-all-start.3 = ((bf16[4,1,128,512]{3,2,1,0:T(8,128)(2,1)}), bf16[4,1,128,512]{3,2,1,0:T(8,128)(2,1)S(1)}, u32[]{:S(2)}, u32[]{:S(2)}) async-start(bf16[4,1,128,512]{3,2,1,0:T(8,128)(2,1)} %shard_map.71), calls=%async_computation.3 | async-start | bytes 1048576 | tf_op jit(solution)/shard_map/all_to_all | solution.py:26
  135.6 9.1 %collective-permute-done.21.refs_1_.refs_2_ = bf16[512,768]{1,0:T(8,128)(2,1)} collective-permute-done((bf16[512,768]{1,0:T(8,128)(2,1)}, bf16[512,768]{1,0:T(8,128)(2,1)}, u32[]{:S(2)}, u32[]{:S(2)}) %collective-permute-start.21) | collective-permute-done | bytes 786464 | tf_op jit(solution)/shard_map/ppermute | solution.py:21
  146.6 3.6 %collective-permute-done.25.refs_0_.refs_1_ = bf16[512,768]{1,0:T(8,128)(2,1)S(1)} collective-permute-done((bf16[512,768]{1,0:T(8,128)(2,1)}, bf16[512,768]{1,0:T(8,128)(2,1)S(1)}, u32[]{:S(2)}, u32[]{:S(2)}) %collective-permute-start.25) | collective-permute-done | bytes 786464 | tf_op jit(solution)/shard_map/ppermute | solution.py:21
  150.2 3.2 %shard_map.73 = bf16[4,2,128,512]{3,2,1,0:T(8,128)(2,1)S(1)} custom-call(bf16[512,768]{1,0:T(8,128)(2,1)S(1)} %copy-done.7, bf16[512,768]{1,0:T(8,128)(2,1)S(1)} %collective-permute-done.25.refs_0_.refs_1_, bf16[512,768]{1,0:T(8,128)(2,1)} %collective-permute-done.21.refs_1_.refs_2_), custom_call_target="tpu_custom_call" | custom-call | flops 1610612736 | bytes 3407872 | tf_op jit(solution)/shard_map/pallas_call | solution.py:260
  154.4 4.3 %all-to-all-start.4 = ((bf16[4,2,128,512]{3,2,1,0:T(8,128)(2,1)}), bf16[4,2,128,512]{3,2,1,0:T(8,128)(2,1)S(1)}, u32[]{:S(2)}, u32[]{:S(2)}) async-start(bf16[4,2,128,512]{3,2,1,0:T(8,128)(2,1)} %copy-done.9), calls=%async_computation.4 | async-start | bytes 2097152 | tf_op jit(solution)/shard_map/all_to_all | solution.py:26
  161.6 13.5 %all-to-all-done.4.blocks_ref = bf16[4,2,128,512]{3,2,1,0:T(8,128)(2,1)S(1)} async-done(((bf16[4,2,128,512]{3,2,1,0:T(8,128)(2,1)}), bf16[4,2,128,512]{3,2,1,0:T(8,128)(2,1)S(1)}, u32[]{:S(2)}, u32[]{:S(2)}) %all-to-all-start.4) | async-done | bytes 1048608 | tf_op jit(solution)/shard_map/all_to_all | solution.py:26
  175.1 4.1 %all-to-all-start.1 = ((bf16[4,1,128,512]{3,2,1,0:T(8,128)(2,1)}), bf16[4,1,128,512]{3,2,1,0:T(8,128)(2,1)}, u32[]{:S(2)}, u32[]{:S(2)}) async-start(bf16[4,1,128,512]{3,2,1,0:T(8,128)(2,1)} %copy-done.12), calls=%async_computation.1 | async-start | bytes 1048576 | tf_op jit(solution)/shard_map/all_to_all | solution.py:26
  179.4 8.2 %collective-permute-start.26 = (bf16[2,128,512]{2,1,0:T(8,128)(2,1)S(1)}, bf16[2,128,512]{2,1,0:T(8,128)(2,1)S(1)}, u32[]{:S(2)}, u32[]{:S(2)}) collective-permute-start(bf16[2,128,512]{2,1,0:T(8,128)(2,1)S(1)} %shard_map.74.refs_2_), channel_id=1, source_target_pairs={{0,1},{1,0},{2,3},{3,2},{4,5},{5,4},{6,7},{7,6},{8,9},{9,8},{10,11... | collective-permute-start | bytes 786440 | tf_op jit(solution)/shard_map/ppermute | solution.py:31
  187.7 6.3 %collective-permute-start.24 = (bf16[1,128,512]{2,1,0:T(8,128)(2,1)S(1)}, bf16[1,128,512]{2,1,0:T(8,128)(2,1)S(1)}, u32[]{:S(2)}, u32[]{:S(2)}) collective-permute-start(bf16[1,128,512]{2,1,0:T(8,128)(2,1)S(1)} %shard_map.72.refs_0_), channel_id=1, source_target_pairs={{0,1},{1,0},{2,3},{3,2},{4,5},{5,4},{6,7},{7,6},{8,9},{9,8},{10,11... | collective-permute-start | bytes 393224 | tf_op jit(solution)/shard_map/ppermute | solution.py:31
  194.2 32.3 %collective-permute-done.24.refs_1_ = bf16[1,128,512]{2,1,0:T(8,128)(2,1)S(1)} collective-permute-done((bf16[1,128,512]{2,1,0:T(8,128)(2,1)S(1)}, bf16[1,128,512]{2,1,0:T(8,128)(2,1)S(1)}, u32[]{:S(2)}, u32[]{:S(2)}) %collective-permute-start.24) | collective-permute-done | bytes 131104 | tf_op jit(solution)/shard_map/ppermute | solution.py:31
  228.5 4.5 %all-to-all-start.5 = ((bf16[4,3,128,512]{3,2,1,0:T(8,128)(2,1)}), bf16[4,3,128,512]{3,2,1,0:T(8,128)(2,1)S(1)}, u32[]{:S(2)}, u32[]{:S(2)}) async-start(bf16[4,3,128,512]{3,2,1,0:T(8,128)(2,1)} %copy-done.4), calls=%async_computation.5 | async-start | bytes 3145728 | tf_op jit(solution)/shard_map/all_to_all | solution.py:26
  234.0 8.4 %collective-permute-start.23 = (bf16[1,128,512]{2,1,0:T(8,128)(2,1)S(1)}, bf16[1,128,512]{2,1,0:T(8,128)(2,1)S(1)}, u32[]{:S(2)}, u32[]{:S(2)}) collective-permute-start(bf16[1,128,512]{2,1,0:T(8,128)(2,1)S(1)} %shard_map.69.refs_0_), channel_id=1, source_target_pairs={{0,1},{1,0},{2,3},{3,2},{4,5},{5,4},{6,7},{7,6},{8,9},{9,8},{10,11... | collective-permute-start | bytes 393224 | tf_op jit(solution)/shard_map/ppermute | solution.py:31
  242.4 9.0 %collective-permute-done.23.refs_1_ = bf16[1,128,512]{2,1,0:T(8,128)(2,1)S(1)} collective-permute-done((bf16[1,128,512]{2,1,0:T(8,128)(2,1)S(1)}, bf16[1,128,512]{2,1,0:T(8,128)(2,1)S(1)}, u32[]{:S(2)}, u32[]{:S(2)}) %collective-permute-start.23) | collective-permute-done | bytes 131104 | tf_op jit(solution)/shard_map/ppermute | solution.py:31
  252.9 4.5 %all-to-all-start.2 = ((bf16[4,1,128,512]{3,2,1,0:T(8,128)(2,1)}), bf16[4,1,128,512]{3,2,1,0:T(8,128)(2,1)}, u32[]{:S(2)}, u32[]{:S(2)}) async-start(bf16[4,1,128,512]{3,2,1,0:T(8,128)(2,1)} %copy-done.8), calls=%async_computation.2 | async-start | bytes 1048576 | tf_op jit(solution)/shard_map/all_to_all | solution.py:26
  258.5 3.8 %shard_map.76.refs_1_ = f32[512,768]{1,0:T(8,128)} custom-call(bf16[4,3,128,512]{3,2,1,0:T(8,128)(2,1)S(1)} %all-to-all-done.5.amplitude_ref, bf16[512,768]{1,0:T(8,128)(2,1)S(1)} %copy-done.7, bf16[512,768]{1,0:T(8,128)(2,1)S(1)} %copy-done.11, bf16[512,768]{1,0:T(8,128)(2,1)} %collective-permute-done.21.refs_1_.refs_2_), custom_call_target="tpu_custom_call" | custom-call | flops 1207959552 | bytes 5505024 | tf_op jit(solution)/shard_map/pallas_call | solution.py:359
  262.3 4.7 %all-to-all-done.2.amplitude_ref = bf16[4,1,128,512]{3,2,1,0:T(8,128)(2,1)} async-done(((bf16[4,1,128,512]{3,2,1,0:T(8,128)(2,1)}), bf16[4,1,128,512]{3,2,1,0:T(8,128)(2,1)}, u32[]{:S(2)}, u32[]{:S(2)}) %all-to-all-start.2) | async-done | bytes 524320 | tf_op jit(solution)/shard_map/all_to_all | solution.py:26
  267.0 4.4 %shard_map.77 = f32[512,768]{1,0:T(8,128)} custom-call(bf16[4,1,128,512]{3,2,1,0:T(8,128)(2,1)} %all-to-all-done.2.amplitude_ref, bf16[512,768]{1,0:T(8,128)(2,1)} %collective-permute-done.22.refs_0_, f32[512,768]{1,0:T(8,128)} %shard_map.76.refs_1_), custom_call_target="tpu_custom_call", output_to_operand_aliasing={{}: (2, {})} | custom-call | flops 402653184 | bytes 2883584 | tf_op jit(solution)/shard_map/pallas_call | solution.py:359
  (112 shorter events, 47.6 us)
Async XLA Ops:
  0.0 88.4 %copy-start = (bf16[768,512]{1,0:T(8,128)(2,1)S(1)}, bf16[768,512]{1,0:T(8,128)(2,1)}, u32[]{:S(2)}) copy-start(bf16[768,512]{1,0:T(8,128)(2,1)} %param.11) | copy-start | bytes 2359300
  2.8 113.4 %all-to-all-start = ((bf16[64,8,768]{2,1,0:T(8,128)(2,1)}), bf16[64,8,768]{2,1,0:T(8,128)(2,1)}, u32[]{:S(2)}, u32[]{:S(2)}) async-start(bf16[64,8,768]{2,1,0:T(8,128)(2,1)} %copy-done.5), calls=%async_computation | async-start | bytes 1572864 | tf_op jit(solution)/shard_map/all_to_all | solution.py:238
  19.8 18.5 %copy-start.24 = (s32[64]{0:T(128)S(1)}, s32[64]{0:T(128)}, u32[]{:S(2)}) copy-start(s32[64]{0:T(128)} %param.10) | copy-start | bytes 772
  22.2 17.0 %collective-permute-start.10 = (bf16[8,16,768]{2,1,0:T(8,128)(2,1)S(1)}, bf16[8,16,768]{2,1,0:T(8,128)(2,1)S(1)}, u32[]{:S(2)}, u32[]{:S(2)}) collective-permute-start(bf16[8,16,768]{2,1,0:T(8,128)(2,1)S(1)} %get-tuple-element.31), channel_id=1, source_target_pairs={{0,32},{8,40},{16,48},{24,56},{32,0},{40,8},{48,16},{56,24},{64,96... | collective-permute-start | bytes 589832 | tf_op jit(solution)/shard_map/ppermute | solution.py:36
  25.6 15.6 %collective-permute-start.11 = (bf16[8,16,768]{2,1,0:T(8,128)(2,1)S(1)}, bf16[8,16,768]{2,1,0:T(8,128)(2,1)S(1)}, u32[]{:S(2)}, u32[]{:S(2)}) collective-permute-start(bf16[8,16,768]{2,1,0:T(8,128)(2,1)S(1)} %get-tuple-element.32), channel_id=1, source_target_pairs={{0,40},{8,32},{16,56},{24,48},{32,8},{40,0},{48,24},{56,16},{64,10... | collective-permute-start | bytes 589832 | tf_op jit(solution)/shard_map/ppermute | solution.py:36
  29.0 17.5 %collective-permute-start.12 = (bf16[8,16,768]{2,1,0:T(8,128)(2,1)S(1)}, bf16[8,16,768]{2,1,0:T(8,128)(2,1)S(1)}, u32[]{:S(2)}, u32[]{:S(2)}) collective-permute-start(bf16[8,16,768]{2,1,0:T(8,128)(2,1)S(1)} %get-tuple-element.33), channel_id=1, source_target_pairs={{0,48},{8,56},{16,32},{24,40},{32,16},{40,24},{48,0},{56,8},{64,11... | collective-permute-start | bytes 589832 | tf_op jit(solution)/shard_map/ppermute | solution.py:36
  31.5 17.7 %collective-permute-start.13 = (bf16[8,16,768]{2,1,0:T(8,128)(2,1)S(1)}, bf16[8,16,768]{2,1,0:T(8,128)(2,1)S(1)}, u32[]{:S(2)}, u32[]{:S(2)}) collective-permute-start(bf16[8,16,768]{2,1,0:T(8,128)(2,1)S(1)} %get-tuple-element.34), channel_id=1, source_target_pairs={{0,56},{8,48},{16,40},{24,32},{32,24},{40,16},{48,8},{56,0},{64,12... | collective-permute-start | bytes 589832 | tf_op jit(solution)/shard_map/ppermute | solution.py:36
  36.1 13.1 %collective-permute-start.7 = (bf16[8,16,768]{2,1,0:T(8,128)(2,1)S(1)}, bf16[8,16,768]{2,1,0:T(8,128)(2,1)S(1)}, u32[]{:S(2)}, u32[]{:S(2)}) collective-permute-start(bf16[8,16,768]{2,1,0:T(8,128)(2,1)S(1)} %get-tuple-element.28), channel_id=1, source_target_pairs={{0,8},{8,0},{16,24},{24,16},{32,40},{40,32},{48,56},{56,48},{64,72... | collective-permute-start | bytes 589832 | tf_op jit(solution)/shard_map/ppermute | solution.py:36
  39.2 10.0 %collective-permute-start.8 = (bf16[8,16,768]{2,1,0:T(8,128)(2,1)S(1)}, bf16[8,16,768]{2,1,0:T(8,128)(2,1)S(1)}, u32[]{:S(2)}, u32[]{:S(2)}) collective-permute-start(bf16[8,16,768]{2,1,0:T(8,128)(2,1)S(1)} %get-tuple-element.29), channel_id=1, source_target_pairs={{0,16},{8,24},{16,0},{24,8},{32,48},{40,56},{48,32},{56,40},{64,80... | collective-permute-start | bytes 589832 | tf_op jit(solution)/shard_map/ppermute | solution.py:36
  41.2 11.8 %collective-permute-start.9 = (bf16[8,16,768]{2,1,0:T(8,128)(2,1)S(1)}, bf16[8,16,768]{2,1,0:T(8,128)(2,1)S(1)}, u32[]{:S(2)}, u32[]{:S(2)}) collective-permute-start(bf16[8,16,768]{2,1,0:T(8,128)(2,1)S(1)} %get-tuple-element.30), channel_id=1, source_target_pairs={{0,24},{8,16},{16,8},{24,0},{32,56},{40,48},{48,40},{56,32},{64,88... | collective-permute-start | bytes 589832 | tf_op jit(solution)/shard_map/ppermute | solution.py:36
  56.3 20.4 %collective-permute-start.14 = (bf16[88,768]{1,0:T(8,128)(2,1)S(1)}, bf16[88,768]{1,0:T(8,128)(2,1)S(1)}, u32[]{:S(2)}, u32[]{:S(2)}) collective-permute-start(bf16[88,768]{1,0:T(8,128)(2,1)S(1)} %get-tuple-element.36), channel_id=1, source_target_pairs={{0,64},{8,72},{16,80},{24,88},{32,96},{40,104},{48,112},{56,120},{... | collective-permute-start | bytes 405512 | tf_op jit(solution)/shard_map/ppermute | solution.py:36
  59.2 25.8 %collective-permute-start.15 = (bf16[88,768]{1,0:T(8,128)(2,1)S(1)}, bf16[88,768]{1,0:T(8,128)(2,1)S(1)}, u32[]{:S(2)}, u32[]{:S(2)}) collective-permute-start(bf16[88,768]{1,0:T(8,128)(2,1)S(1)} %get-tuple-element.37), channel_id=1, source_target_pairs={{0,128},{8,136},{16,144},{24,152},{32,160},{40,168},{48,176},{56,1... | collective-permute-start | bytes 405512 | tf_op jit(solution)/shard_map/ppermute | solution.py:36
  63.9 27.1 %collective-permute-start.16 = (bf16[88,768]{1,0:T(8,128)(2,1)S(1)}, bf16[88,768]{1,0:T(8,128)(2,1)S(1)}, u32[]{:S(2)}, u32[]{:S(2)}) collective-permute-start(bf16[88,768]{1,0:T(8,128)(2,1)S(1)} %get-tuple-element.38), channel_id=1, source_target_pairs={{0,192},{8,200},{16,208},{24,216},{32,224},{40,232},{48,240},{56,2... | collective-permute-start | bytes 405512 | tf_op jit(solution)/shard_map/ppermute | solution.py:36
  66.4 38.3 %collective-permute-start.17 = (bf16[88,768]{1,0:T(8,128)(2,1)S(1)}, bf16[88,768]{1,0:T(8,128)(2,1)S(1)}, u32[]{:S(2)}, u32[]{:S(2)}) collective-permute-start(bf16[88,768]{1,0:T(8,128)(2,1)S(1)} %get-tuple-element.39), channel_id=1, source_target_pairs={{0,256},{8,264},{16,272},{24,280},{32,288},{40,296},{48,304},{56,3... | collective-permute-start | bytes 405512 | tf_op jit(solution)/shard_map/ppermute | solution.py:36
  73.6 42.6 %collective-permute-start.18 = (bf16[88,768]{1,0:T(8,128)(2,1)S(1)}, bf16[88,768]{1,0:T(8,128)(2,1)S(1)}, u32[]{:S(2)}, u32[]{:S(2)}) collective-permute-start(bf16[88,768]{1,0:T(8,128)(2,1)S(1)} %get-tuple-element.40), channel_id=1, source_target_pairs={{0,320},{8,328},{16,336},{24,344},{32,352},{40,360},{48,368},{56,3... | collective-permute-start | bytes 405512 | tf_op jit(solution)/shard_map/ppermute | solution.py:36
  76.8 39.4 %collective-permute-start.19 = (bf16[88,768]{1,0:T(8,128)(2,1)S(1)}, bf16[88,768]{1,0:T(8,128)(2,1)S(1)}, u32[]{:S(2)}, u32[]{:S(2)}) collective-permute-start(bf16[88,768]{1,0:T(8,128)(2,1)S(1)} %get-tuple-element.41), channel_id=1, source_target_pairs={{0,384},{8,392},{16,400},{24,408},{32,416},{40,424},{48,432},{56,4... | collective-permute-start | bytes 405512 | tf_op jit(solution)/shard_map/ppermute | solution.py:36
  85.0 31.2 %collective-permute-start.20 = (bf16[88,768]{1,0:T(8,128)(2,1)S(1)}, bf16[88,768]{1,0:T(8,128)(2,1)S(1)}, u32[]{:S(2)}, u32[]{:S(2)}) collective-permute-start(bf16[88,768]{1,0:T(8,128)(2,1)S(1)} %get-tuple-element.42), channel_id=1, source_target_pairs={{0,448},{8,456},{16,464},{24,472},{32,480},{40,488},{48,496},{56,5... | collective-permute-start | bytes 405512 | tf_op jit(solution)/shard_map/ppermute | solution.py:36
  91.0 25.2 %copy-start.19 = (bf16[88,768]{1,0:T(8,128)(2,1)}, bf16[88,768]{1,0:T(8,128)(2,1)S(1)}, u32[]{:S(2)}) copy-start(bf16[88,768]{1,0:T(8,128)(2,1)S(1)} %collective-permute-done.16.refs_3_) | copy-start | bytes 405508
  121.3 23.3 %collective-permute-start.21 = (bf16[512,768]{1,0:T(8,128)(2,1)}, bf16[512,768]{1,0:T(8,128)(2,1)}, u32[]{:S(2)}, u32[]{:S(2)}) collective-permute-start(bf16[512,768]{1,0:T(8,128)(2,1)} %shard_map.67.own_ref.refs_0_), channel_id=1, source_target_pairs={{0,16},{8,24},{16,32},{24,40},{32,48},{40,56},{48,64},{56,72},{64,... | collective-permute-start | bytes 2359304 | tf_op jit(solution)/shard_map/ppermute | solution.py:21
  126.4 23.7 %collective-permute-start.25 = (bf16[512,768]{1,0:T(8,128)(2,1)}, bf16[512,768]{1,0:T(8,128)(2,1)S(1)}, u32[]{:S(2)}, u32[]{:S(2)}) collective-permute-start(bf16[512,768]{1,0:T(8,128)(2,1)} %shard_map.67.own_ref.refs_0_), channel_id=1, source_target_pairs={{0,8},{8,16},{16,24},{24,32},{32,40},{40,48},{48,56},{56,64},{64,7... | collective-permute-start | bytes 2359304 | tf_op jit(solution)/shard_map/ppermute | solution.py:21
  129.5 20.7 %copy-start.7 = (bf16[512,768]{1,0:T(8,128)(2,1)S(1)}, bf16[512,768]{1,0:T(8,128)(2,1)}, u32[]{:S(2)}) copy-start(bf16[512,768]{1,0:T(8,128)(2,1)} %shard_map.67.own_ref.refs_0_) | copy-start | bytes 2359300
  131.3 23.1 %all-to-all-start.3 = ((bf16[4,1,128,512]{3,2,1,0:T(8,128)(2,1)}), bf16[4,1,128,512]{3,2,1,0:T(8,128)(2,1)S(1)}, u32[]{:S(2)}, u32[]{:S(2)}) async-start(bf16[4,1,128,512]{3,2,1,0:T(8,128)(2,1)} %shard_map.71), calls=%async_computation.3 | async-start | bytes 1048576 | tf_op jit(solution)/shard_map/all_to_all | solution.py:26
  144.7 14.0 %collective-permute-start.22 = (bf16[512,768]{1,0:T(8,128)(2,1)}, bf16[512,768]{1,0:T(8,128)(2,1)}, u32[]{:S(2)}, u32[]{:S(2)}) collective-permute-start(bf16[512,768]{1,0:T(8,128)(2,1)} %collective-permute-done.21.refs_1_.refs_2_), channel_id=1, source_target_pairs={{0,8},{8,16},{16,24},{24,32},{32,40},{40,48},{48,56},{56,64},{64,7... | collective-permute-start | bytes 2359304 | tf_op jit(solution)/shard_map/ppermute | solution.py:21
  154.4 20.7 %all-to-all-start.4 = ((bf16[4,2,128,512]{3,2,1,0:T(8,128)(2,1)}), bf16[4,2,128,512]{3,2,1,0:T(8,128)(2,1)S(1)}, u32[]{:S(2)}, u32[]{:S(2)}) async-start(bf16[4,2,128,512]{3,2,1,0:T(8,128)(2,1)} %copy-done.9), calls=%async_computation.4 | async-start | bytes 2097152 | tf_op jit(solution)/shard_map/all_to_all | solution.py:26
  161.6 32.4 %copy-start.14 = (f32[512]{0:T(512)S(1)}, f32[512]{0:T(512)}, u32[]{:S(2)}) copy-start(f32[512]{0:T(512)} %param.13) | copy-start | bytes 6148
  161.6 64.8 %copy-start.16 = (f32[64]{0:T(128)S(1)}, f32[64]{0:T(128)}, u32[]{:S(2)}) copy-start(f32[64]{0:T(128)} %energy_ref.3) | copy-start | bytes 772
  175.1 53.3 %all-to-all-start.1 = ((bf16[4,1,128,512]{3,2,1,0:T(8,128)(2,1)}), bf16[4,1,128,512]{3,2,1,0:T(8,128)(2,1)}, u32[]{:S(2)}, u32[]{:S(2)}) async-start(bf16[4,1,128,512]{3,2,1,0:T(8,128)(2,1)} %copy-done.12), calls=%async_computation.1 | async-start | bytes 1048576 | tf_op jit(solution)/shard_map/all_to_all | solution.py:26
  179.4 47.1 %collective-permute-start.26 = (bf16[2,128,512]{2,1,0:T(8,128)(2,1)S(1)}, bf16[2,128,512]{2,1,0:T(8,128)(2,1)S(1)}, u32[]{:S(2)}, u32[]{:S(2)}) collective-permute-start(bf16[2,128,512]{2,1,0:T(8,128)(2,1)S(1)} %shard_map.74.refs_2_), channel_id=1, source_target_pairs={{0,1},{1,0},{2,3},{3,2},{4,5},{5,4},{6,7},{7,6},{8,9},{9,8},{10,11... | collective-permute-start | bytes 786440 | tf_op jit(solution)/shard_map/ppermute | solution.py:31
  187.7 38.8 %collective-permute-start.24 = (bf16[1,128,512]{2,1,0:T(8,128)(2,1)S(1)}, bf16[1,128,512]{2,1,0:T(8,128)(2,1)S(1)}, u32[]{:S(2)}, u32[]{:S(2)}) collective-permute-start(bf16[1,128,512]{2,1,0:T(8,128)(2,1)S(1)} %shard_map.72.refs_0_), channel_id=1, source_target_pairs={{0,1},{1,0},{2,3},{3,2},{4,5},{5,4},{6,7},{7,6},{8,9},{9,8},{10,11... | collective-permute-start | bytes 393224 | tf_op jit(solution)/shard_map/ppermute | solution.py:31
  228.5 24.4 %all-to-all-start.5 = ((bf16[4,3,128,512]{3,2,1,0:T(8,128)(2,1)}), bf16[4,3,128,512]{3,2,1,0:T(8,128)(2,1)S(1)}, u32[]{:S(2)}, u32[]{:S(2)}) async-start(bf16[4,3,128,512]{3,2,1,0:T(8,128)(2,1)} %copy-done.4), calls=%async_computation.5 | async-start | bytes 3145728 | tf_op jit(solution)/shard_map/all_to_all | solution.py:26
  234.0 17.3 %collective-permute-start.23 = (bf16[1,128,512]{2,1,0:T(8,128)(2,1)S(1)}, bf16[1,128,512]{2,1,0:T(8,128)(2,1)S(1)}, u32[]{:S(2)}, u32[]{:S(2)}) collective-permute-start(bf16[1,128,512]{2,1,0:T(8,128)(2,1)S(1)} %shard_map.69.refs_0_), channel_id=1, source_target_pairs={{0,1},{1,0},{2,3},{3,2},{4,5},{5,4},{6,7},{7,6},{8,9},{9,8},{10,11... | collective-permute-start | bytes 393224 | tf_op jit(solution)/shard_map/ppermute | solution.py:31
  252.9 14.1 %all-to-all-start.2 = ((bf16[4,1,128,512]{3,2,1,0:T(8,128)(2,1)}), bf16[4,1,128,512]{3,2,1,0:T(8,128)(2,1)}, u32[]{:S(2)}, u32[]{:S(2)}) async-start(bf16[4,1,128,512]{3,2,1,0:T(8,128)(2,1)} %copy-done.8), calls=%async_computation.2 | async-start | bytes 1048576 | tf_op jit(solution)/shard_map/all_to_all | solution.py:26
  (19 other events, 83.0 us)
